TPU v7x, 32 devices: a whole 2x2x4 slice. The times are simulated.
32 devices in a mesh: grp: 2 (over y), loan: 4 (over z), feat: 4 (over x, core).
Axes of the slice: x: 2, y: 2, z: 4, core: 2. Of those that a mesh axis runs over, the one named last changes fastest.
Arguments:
- design: bfloat16 [16384, 4096], P(('grp', 'loan'), 'feat'), parts along dimension 0, may hold values from -6 to 6
- labels: int32 [16384], P(('grp', 'loan')), parts along dimension 0, may hold values from 0 to 1
- pool_ids: int32 [16384], P(('grp', 'loan')), parts along dimension 0, may hold values from 0 to 255, as said below
- pool_region_index: int32 [512], P(('grp', 'loan')), parts along dimension 0, may hold values from 0 to 63
- step_size: float32 [32], P('grp'), parts along dimension 0, may hold values from 0.005 to 0.02
- beta: float32 [32, 4096], P('grp', 'feat'), parts along dimension 0, may hold values from -0.09375 to 0.09375
- pools: float32 [32, 256, 256], P('grp', 'loan', 'feat'), parts along dimension 0, may hold values from -0.5 to 0.5
- regions: float32 [32, 64, 256], P('grp', None, 'feat'), parts along dimension 0, may hold values from -0.5 to 0.5
- beta_momentum: float32 [32, 4096], P('grp', 'feat'), parts along dimension 0, may hold values from -6 to 6
- pool_momentum: float32 [32, 256, 256], P('grp', 'loan', 'feat'), parts along dimension 0, may hold values from -6 to 6
- region_momentum: float32 [32, 64, 256], P('grp', None, 'feat'), parts along dimension 0, may hold values from -6 to 6
Outputs:
- beta_next: float32 [32, 4096], P('grp', 'feat'), parts along dimension 0
- pools_next: float32 [32, 256, 256], P('grp', 'loan', 'feat'), parts along dimension 0
- regions_next: float32 [32, 64, 256], P('grp', None, 'feat'), parts along dimension 0
- beta_momentum_next: float32 [32, 4096], P('grp', 'feat'), parts along dimension 0
- pool_momentum_next: float32 [32, 256, 256], P('grp', 'loan', 'feat'), parts along dimension 0
- region_momentum_next: float32 [32, 64, 256], P('grp', None, 'feat'), parts along dimension 0
There are 2 independent parts, one for each index of `grp`. A program takes and returns all parts, laid end to end along the dimension named above; each array names one. Nothing has to cross between parts.
Inputs may be any that keep to these rules, and one draw needn't show every extreme that they name: `pool_ids`: in each aligned block of 2048 loans (block l counted from 0) the pool ids lie in l * 64 to (l + 1) * 64 - 1 and do not fall along the block.
All inputs are finite; a program needn't handle non-finite values.
Results may differ from a plain program's by a relative error of at most 0.0006.
Values may be sent and summed in bfloat16 or wider, within the bound.
A program may use at most 64 MiB of HBM per device.

v0:
```python
import jax
import jax.numpy as jnp
from jax import lax
from jax.sharding import PartitionSpec as P

F = 4096
G = 256


MATMUL_ACCURACY = 256.0


def gradient(
    design, labels, pool_ids, pool_region_index, b_full, b_own, upper_operand, lower_operand
):
    stride = F // G
    slope_bf = design[:, ::stride]
    slope_feats = slope_bf.astype(jnp.float32)
    rows = design.shape[0]
    owned = upper_operand.shape[1]
    first = lax.axis_index("loan") * owned
    local_ids = pool_ids - first
    b16 = b_full.astype(jnp.bfloat16)
    linear = lax.dot_general(
        b16, design, (((1,), (1,)), ((), ())), preferred_element_type=jnp.float32
    )
    chosen = jnp.take(upper_operand, local_ids, axis=1)
    term = jnp.einsum("ng,cng->cn", slope_feats, chosen, precision=lax.Precision.HIGHEST)
    partial_logit = linear + term
    width = rows // lax.axis_size("feat")
    share = lax.psum_scatter(partial_logit, "feat", scatter_dimension=1, tiled=True)
    mine = lax.dynamic_slice_in_dim(labels, lax.axis_index("feat") * width, width)
    resid_share = (mine.astype(jnp.float32)[None, :] - jax.nn.sigmoid(share)).astype(jnp.bfloat16)
    resid = lax.all_gather(resid_share, "feat", axis=1, tiled=True)
    xt = lax.dot_general(
        resid, design, (((1,), (0,)), ((), ())), preferred_element_type=jnp.float32
    )
    member = (local_ids[:, None] == jnp.arange(owned, dtype=jnp.int32)[None, :]).astype(
        jnp.bfloat16
    )
    resid_table = resid[:, :, None] * member[None, :, :]
    lik = jnp.einsum("cnp,ng->cpg", resid_table, slope_bf, preferred_element_type=jnp.float32)
    region_lookup_matrix = (
        pool_region_index[:, None] == jnp.arange(lower_operand.shape[1], dtype=jnp.int32)[None, :]
    ).astype(jnp.float32)
    selected_operand = jnp.einsum(
        "bv,yva->yba", region_lookup_matrix, lower_operand, precision=lax.Precision.HIGHEST
    )
    device_index = MATMUL_ACCURACY * (upper_operand - selected_operand)
    gu = lik - device_index
    region_part = jnp.einsum(
        "pr,cpg->crg", region_lookup_matrix, device_index, precision=lax.Precision.HIGHEST
    )
    xt_total, region_total = lax.psum((xt, region_part), "loan")
    gb = xt_total - F * b_own
    gv = region_total - MATMUL_ACCURACY * lower_operand
    return (gb, gu, gv)


def body(
    design,
    labels,
    pool_ids,
    pool_region_index,
    step_size,
    beta,
    pools,
    regions,
    beta_momentum,
    pool_momentum,
    region_momentum,
):
    half = 0.5 * step_size
    h2 = half[:, None]
    h3 = half[:, None, None]
    e2 = step_size[:, None]
    e3 = step_size[:, None, None]
    gb, gu, gv = gradient(design, labels, pool_ids, pool_region_index, beta, beta, pools, regions)
    mb = beta_momentum + h2 * gb
    mu = pool_momentum + h3 * gu
    mv = region_momentum + h3 * gv
    beta_next_own = beta + e2 * mb
    pools_next = pools + e3 * mu
    regions_next = regions + e3 * mv
    gb, gu, gv = gradient(
        design,
        labels,
        pool_ids,
        pool_region_index,
        beta_next_own,
        beta_next_own,
        pools_next,
        regions_next,
    )
    mb_next = mb + h2 * gb
    return (beta_next_own, pools_next, regions_next, mb_next, mu + h3 * gu, mv + h3 * gv)


def solution(mesh):
    in_specs = (
        P(("grp", "loan"), "feat"),
        P(("grp", "loan")),
        P(("grp", "loan")),
        P(("grp", "loan")),
        P("grp"),
        P("grp", "feat"),
        P("grp", "loan", "feat"),
        P("grp", None, "feat"),
        P("grp", "feat"),
        P("grp", "loan", "feat"),
        P("grp", None, "feat"),
    )
    out_specs = (
        P("grp", "feat"),
        P("grp", "loan", "feat"),
        P("grp", None, "feat"),
        P("grp", "feat"),
        P("grp", "loan", "feat"),
        P("grp", None, "feat"),
    )
    return jax.shard_map(body, mesh=mesh, in_specs=in_specs, out_specs=out_specs, check_vma=False)
```

profile of v0, /device:TPU:0, one launch (start us, length us, event | category | flops | bytes accessed | tf_op | source)
XLA Modules:
  0.0 294.6 jit_solution(9873602378691993713)
XLA Ops:
  7.2 0.0 copy-start
  7.2 0.0 reduce-scatter.3.cloned.1.call-start
  7.2 0.8 compare_and_fusion
  8.0 11.7 %slice.4 = bf16[2048,64]{1,0:T(8,128)(2,1)S(1)} slice(bf16[2048,1024]{1,0:T(8,128)(2,1)} %param.13), slice={[0:2048:1], [0:1024:16]} | slice | bytes 524288 | tf_op jit(solution)/shard_map/slice | solution.py:17
  19.7 0.2 copy.48
  19.9 0.2 copy.49
  20.1 50.2 %gather_fusion = f32[2048,16,64]{2,0,1:T(8,128)} fusion(f32[16,64,64]{2,1,0:T(8,128)S(1)} %copy-done, s32[2048]{0:T(1024)S(1)} %fusion.46), kind=kCustom, calls=%fused_computation.clone | custom fusion | bytes 16785408 | tf_op jit(solution)/shard_map/jit(_take)/gather | solution.py:27
  70.3 9.0 %fusion.1 = f32[2048,16]{0,1:T(8,128)S(1)} fusion(f32[2048,16,64]{2,0,1:T(8,128)} %gather_fusion, f32[2048,64]{1,0:T(8,128)S(1)} %copy.49, pred[2048]{0:T(1024)(128)(4,1)S(1)} %get-tuple-element.11), kind=kLoop, calls=%fused_computation.5 | loop fusion | flops 6258688 | bytes 9046016 | tf_op jit(solution)/shard_map/ng,cng->cn/dot_general | solution.py:28
  79.3 0.0 copy-start.4
  79.3 0.0 copy-start.17
  79.4 1.9 convolution_add_fusion.1
  81.2 0.0 reduce-scatter.3.cloned.1.call-update
  81.2 0.0 all-reduce.7.cloned.1.call-start
  81.3 0.4 fusion.29
  81.7 0.8 dynamic-slice_convert_fusion
  82.5 1.3 convolution_bitcast_fusion.2
  83.8 20.0 %reduce-scatter.3.cloned.1.call-done = f32[16,512]{1,0:T(8,128)} async-done(((f32[16,2048]{1,0:T(8,128)}), f32[16,512]{1,0:T(8,128)}) %reduce-scatter.3.cloned.1.call-update) | async-done | bytes 32784 | tf_op jit(solution)/shard_map/reduce_scatter | solution.py:31
  103.8 0.8 subtract_convert_fusion.1
  104.5 5.2 %all_gather.6 = bf16[16,2048]{1,0:T(8,128)(2,1)S(1)} all-gather(bf16[16,512]{1,0:T(8,128)(2,1)S(1)} %subtract_convert_fusion.1), channel_id=1, replica_groups=mesh['grp'=2,'loan'=4,'feat'=4] {'feat'}, dimensions={1}, use_global_device_ids=true | all-gather | bytes 81920 | tf_op jit(solution)/shard_map/all_gather | solution.py:34
  109.8 3.5 %fusion.47 = f32[16,1024]{1,0:T(8,128)} fusion(bf16[16,2048]{1,0:T(8,128)(2,1)S(1)} %all_gather.6, bf16[2048,1024]{1,0:T(8,128)(2,1)} %param.13), kind=kOutput, calls=%fused_computation.57 | convolution fusion | flops 67108864 | bytes 4325376 | tf_op jit(solution)/shard_map/dot_general | solution.py:35
  113.3 0.0 all-reduce.7.cloned.1.call-update
  113.3 0.2 reduce-scatter.5.cloned.1.call-start
  113.6 0.7 broadcast_multiply_fusion
  114.2 38.9 %all-reduce.7.cloned.1.call-done = (f32[16,1024]{1,0:T(8,128)}, f32[16,64,64]{2,1,0:T(8,128)}) async-done(((f32[16,1024]{1,0:T(8,128)}, f32[16,64,64]{2,1,0:T(8,128)}), (f32[16,1024]{1,0:T(8,128)}, f32[16,64,64]{2,1,0:T(8,128)})) %all-reduce.7.cloned.1.call-update) | async-done | bytes 327696 | tf_op jit(solution)/shard_map/psum | solution.py:54
  153.1 3.7 %multiply_add_fusion.1 = (f32[16,64,64]{2,1,0:T(8,128)}, f32[16,64,64]{2,1,0:T(8,128)S(1)}, f32[16,64,64]{2,1,0:T(8,128)}) fusion(f32[16,64,64]{2,1,0:T(8,128)} %param.20, f32[16]{0:T(128)} %param.17, f32[16,64,64]{2,1,0:T(8,128)} %param.23, f32[16,64,64]{2,1,0:T(8,128)} %get-tuple-element.10, f32[16]{0:T(128)S(1)} %broadcast_multiply_fusion, ...), kind=kOutput, calls=%fused_computation.33 | convolution fusion | flops 271253504 | bytes 2949248 | tf_op jit(solution)/shard_map/cnp,ng->cpg/dot_general | solution.py:42
  156.8 0.3 copy.27
  157.1 0.5 copy-done.2
  157.6 20.7 %gather_fusion.1 = f32[2048,16,64]{2,1,0:T(8,128)} fusion(f32[16,64,64]{2,0,1:T(8,128)S(1)} %copy.27, s32[2048]{0:T(1024)S(1)} %fusion.46), kind=kCustom, calls=%fused_computation.1.clone | custom fusion | bytes 16785408 | tf_op jit(solution)/shard_map/jit(_take)/gather | solution.py:27
  178.3 32.8 %fusion = f32[2048,16]{1,0:T(8,128)S(1)} fusion(f32[2048,16,64]{2,1,0:T(8,128)} %gather_fusion.1, f32[2048,64]{1,0:T(8,128)S(1)} %copy.49, pred[2048]{0:T(1024)(128)(4,1)S(1)} %copy-done.14), kind=kLoop, calls=%fused_computation.3 | loop fusion | flops 6258688 | bytes 9046016
  211.1 0.0 copy-start.18
  211.2 0.3 copy.43
  211.5 0.0 copy-done.19
  211.5 0.1 multiply_add_fusion.5
  211.6 0.0 copy-start.8
  211.6 4.1 %convolution_add_fusion = f32[16,2048]{1,0:T(8,128)} fusion(bf16[2048,1024]{1,0:T(8,128)(2,1)} %param.13, f32[2048,16]{0,1:T(8,128)S(1)} %copy.43, f32[16,1024]{1,0:T(8,128)S(1)} %multiply_add_fusion.5), kind=kOutput, calls=%fused_computation.10 | convolution fusion | flops 67158016 | bytes 4521984 | tf_op jit(solution)/shard_map/dot_general | solution.py:24
  215.6 0.0 reduce-scatter.5.cloned.1.call-update
  215.7 0.0 all-reduce.5.cloned.1.call-start
  215.8 0.4 fusion.31
  216.2 1.3 convolution_bitcast_fusion
  217.5 17.5 %reduce-scatter.5.cloned.1.call-done = f32[16,512]{1,0:T(8,128)} async-done(((f32[16,2048]{1,0:T(8,128)}), f32[16,512]{1,0:T(8,128)}) %reduce-scatter.5.cloned.1.call-update) | async-done | bytes 32784 | tf_op jit(solution)/shard_map/reduce_scatter | solution.py:31
  234.9 0.8 subtract_convert_fusion
  235.7 5.2 %all_gather.7 = bf16[16,2048]{1,0:T(8,128)(2,1)S(1)} all-gather(bf16[16,512]{1,0:T(8,128)(2,1)S(1)} %subtract_convert_fusion), channel_id=1, replica_groups=mesh['grp'=2,'loan'=4,'feat'=4] {'feat'}, dimensions={1}, use_global_device_ids=true | all-gather | bytes 81920 | tf_op jit(solution)/shard_map/all_gather | solution.py:34
  240.9 3.5 %fusion.48 = f32[16,1024]{1,0:T(8,128)} fusion(bf16[16,2048]{1,0:T(8,128)(2,1)S(1)} %all_gather.7, bf16[2048,1024]{1,0:T(8,128)(2,1)} %param.13), kind=kOutput, calls=%fused_computation.58 | convolution fusion | flops 67108864 | bytes 4325376 | tf_op jit(solution)/shard_map/dot_general | solution.py:35
  244.4 0.0 all-reduce.5.cloned.1.call-update
  244.4 3.2 %fusion.25 = f32[16,64,64]{2,1,0:T(8,128)} fusion(f32[16,64,64]{2,1,0:T(8,128)} %get-tuple-element.15, f32[16,64,64]{2,1,0:T(8,128)S(1)} %fusion.31, bf16[16,2048]{1,0:T(8,128)(2,1)S(1)} %all_gather.7, bf16[2048,64]{0,1:T(8,128)(2,1)S(1)} %fusion.34, bf16[2048,64]{1,0:T(8,128)(2,1)S(1)} %slice.4, f32[16]{0:T(128)S(1)} %broadcast_multiply_fusion), kind=kOutput, calls=%fused_computation.21 | convolution fusion | flops 270729216 | bytes 1376320 | tf_op jit(solution)/shard_map/cnp,ng->cpg/dot_general | solution.py:42
  247.6 36.7 %all-reduce.5.cloned.1.call-done = (f32[16,1024]{1,0:T(8,128)}, f32[16,64,64]{2,1,0:T(8,128)}) async-done(((f32[16,1024]{1,0:T(8,128)}, f32[16,64,64]{2,1,0:T(8,128)}), (f32[16,1024]{1,0:T(8,128)}, f32[16,64,64]{2,1,0:T(8,128)})) %all-reduce.5.cloned.1.call-update) | async-done | bytes 327696 | tf_op jit(solution)/shard_map/psum | solution.py:54
  284.3 1.5 multiply_add_fusion.4
  285.9 2.2 multiply_add_fusion
  (35 shorter events, 0.1 us)
Async XLA Ops:
  7.2 12.9 %copy-start = (f32[16,64,64]{2,1,0:T(8,128)S(1)}, f32[16,64,64]{2,1,0:T(8,128)}, u32[]{:S(2)}) copy-start(f32[16,64,64]{2,1,0:T(8,128)} %param.19) | copy-start | bytes 786436
  7.2 96.6 %reduce-scatter.3.cloned.1.call-start = ((), (), s32[]{:S(2)}) async-start(), calls=%async_computation.2 | async-start | bytes 163840 | tf_op jit(solution)/shard_map/reduce_scatter | solution.py:31
  8.0 62.4 %copy-start.13 = (pred[2048]{0:T(1024)(128)(4,1)}, pred[2048]{0:T(1024)(128)(4,1)S(1)}, u32[]{:S(2)}) copy-start(pred[2048]{0:T(1024)(128)(4,1)S(1)} %get-tuple-element.11) | copy-start | bytes 6148
  70.3 9.0 %copy-start.1 = (bf16[2048,1024]{1,0:T(8,128)(2,1)S(1)}, bf16[2048,1024]{1,0:T(8,128)(2,1)}, u32[]{:S(2)}) copy-start(bf16[2048,1024]{1,0:T(8,128)(2,1)} %param.13) | copy-start | bytes 12582916
  70.3 9.0 %copy-start.7 = (f32[16,1024]{1,0:T(8,128)S(1)}, f32[16,1024]{1,0:T(8,128)}, u32[]{:S(2)}) copy-start(f32[16,1024]{1,0:T(8,128)} %param.18) | copy-start | bytes 196612
  79.3 2.0 copy-start.4
  79.3 2.0 copy-start.17
  81.2 71.9 %all-reduce.7.cloned.1.call-start = ((), (), s32[]{:S(2)}) async-start(), calls=%async_computation.5 | async-start | bytes 1179648 | tf_op jit(solution)/shard_map/psum | solution.py:54
  82.5 21.3 %copy-start.15 = (f32[512]{0:T(512)}, f32[512]{0:T(512)S(1)}, u32[]{:S(2)}) copy-start(f32[512]{0:T(512)S(1)} %dynamic-slice_convert_fusion) | copy-start | bytes 6148
  113.3 121.6 %reduce-scatter.5.cloned.1.call-start = ((), (), s32[]{:S(2)}) async-start(), calls=%async_computation.3 | async-start | bytes 163840 | tf_op jit(solution)/shard_map/reduce_scatter | solution.py:31
  156.8 0.8 copy-start.2
  157.6 20.7 %copy-start.14 = (pred[2048]{0:T(1024)(128)(4,1)S(1)}, pred[2048]{0:T(1024)(128)(4,1)}, u32[]{:S(2)}) copy-start(pred[2048]{0:T(1024)(128)(4,1)} %copy-done.13) | copy-start | bytes 6148
  178.3 33.1 %copy-start.10 = (f32[16,1024]{1,0:T(8,128)S(1)}, f32[16,1024]{1,0:T(8,128)}, u32[]{:S(2)}) copy-start(f32[16,1024]{1,0:T(8,128)} %param.21) | copy-start | bytes 196612
  178.3 33.1 %copy-start.11 = (f32[16,1024]{1,0:T(8,128)S(1)}, f32[16,1024]{1,0:T(8,128)}, u32[]{:S(2)}) copy-start(f32[16,1024]{1,0:T(8,128)} %get-tuple-element.9) | copy-start | bytes 196612
  178.3 33.1 %copy-start.19 = (f32[16]{0:T(128)S(1)}, f32[16]{0:T(128)}, u32[]{:S(2)}) copy-start(f32[16]{0:T(128)} %param.17) | copy-start | bytes 196
  211.1 4.6 %copy-start.3 = (f32[16,64,64]{2,1,0:T(8,128)S(1)}, f32[16,64,64]{2,1,0:T(8,128)}, u32[]{:S(2)}) copy-start(f32[16,64,64]{2,1,0:T(8,128)} %copy-done.2) | copy-start | bytes 786436
  211.1 4.6 %copy-start.6 = (f32[16,64,64]{2,1,0:T(8,128)S(1)}, f32[16,64,64]{2,1,0:T(8,128)}, u32[]{:S(2)}) copy-start(f32[16,64,64]{2,1,0:T(8,128)} %get-tuple-element.13) | copy-start | bytes 786436
  211.1 4.6 %copy-start.18 = (s32[64]{0:T(128)S(1)}, s32[64]{0:T(128)}, u32[]{:S(2)}) copy-start(s32[64]{0:T(128)} %param.16) | copy-start | bytes 772
  211.2 23.8 %copy-start.16 = (f32[512]{0:T(512)S(1)}, f32[512]{0:T(512)}, u32[]{:S(2)}) copy-start(f32[512]{0:T(512)} %copy-done.15) | copy-start | bytes 6148
  211.6 72.8 %copy-start.8 = (f32[16,1024]{1,0:T(8,128)}, f32[16,1024]{1,0:T(8,128)S(1)}, u32[]{:S(2)}) copy-start(f32[16,1024]{1,0:T(8,128)S(1)} %multiply_add_fusion.5) | copy-start | bytes 196612
  215.7 68.6 %all-reduce.5.cloned.1.call-start = ((), (), s32[]{:S(2)}) async-start(), calls=%async_computation.4 | async-start | bytes 1179648 | tf_op jit(solution)/shard_map/psum | solution.py:54
  244.4 39.9 %copy-start.12 = (f32[16,1024]{1,0:T(8,128)S(1)}, f32[16,1024]{1,0:T(8,128)}, u32[]{:S(2)}) copy-start(f32[16,1024]{1,0:T(8,128)} %get-tuple-element.9) | copy-start | bytes 196612
  244.4 41.5 %copy-start.5 = (f32[16,64,64]{2,1,0:T(8,128)S(1)}, f32[16,64,64]{2,1,0:T(8,128)}, u32[]{:S(2)}) copy-start(f32[16,64,64]{2,1,0:T(8,128)} %param.20) | copy-start | bytes 786436
  244.4 41.5 %copy-start.9 = (f32[16,64,64]{2,1,0:T(8,128)S(1)}, f32[16,64,64]{2,1,0:T(8,128)}, u32[]{:S(2)}) copy-start(f32[16,64,64]{2,1,0:T(8,128)} %param.23) | copy-start | bytes 786436
Sparse Core Ops, SparseCore 0:
  81.4 22.3 reduce-scatter.2
  113.4 39.6 all-reduce.6
  215.8 19.0 reduce-scatter.4
  244.6 39.7 all-reduce.4
where the time goes:
time: 295 us
  waiting for transfers between devices  113 us (38%)
  local copies, waits for them, and re-layouts  84.2 us (29%)
  other arithmetic  49.3 us (17%)
  matrix products  23.1 us (8%)
  between operations  14 us (5%)
  blocking collectives  10.5 us (4%)
    psum x2, waiting for transfers between devices, gradient(): xt_total, region_total = lax.psum((xt, region_part), 'loan')  75.6 us
    gather x2, local copies, waits for them, and re-layouts, gradient(): chosen = jnp.take(upper_operand, local_ids, axis=1)  71 us
    reduce_scatter x2, waiting for transfers between devices, gradient(): lax.psum_scatter(partial_logit, 'feat', scatter_dimension=1, tiled=True)  37.4 us
    unnamed x1, other arithmetic  32.8 us
    slice x1, local copies, waits for them, and re-layouts, gradient(): slope_bf = design[:, ::stride]  11.7 us
    all_gather x2, blocking collectives, gradient(): resid = lax.all_gather(resid_share, 'feat', axis=1, tiled=True)  10.5 us
    dot_general x1, other arithmetic, gradient(): jnp.einsum('ng,cng->cn', slope_feats, chosen, precision=lax.Precision.HIG...  8.96 us
    dot_general x2, matrix products, gradient(): lax.dot_general(resid, design, (((1,), (0,)), ((), ())), preferred_elemen...  6.95 us
  transfers between devices with their start and end apart: 4, of which 4 were waited for; matrix products, arithmetic and copies ran while one was open for 3% of the time, Pallas kernels for 0%

commit v1 on v0

v1 whole, which is shorter than its diff:
```python
import functools

import jax
import jax.numpy as jnp
from jax import lax
from jax.experimental import pallas as pl
from jax.experimental.pallas import tpu as pltpu
from jax.sharding import PartitionSpec as P

PREC = 256.0
MESH = pl.DeviceIdType.MESH
NT = (((1,), (1,)), ((), ()))
NN = (((1,), (0,)), ((), ()))
F32 = jnp.float32
BF16 = jnp.bfloat16


def dot(a, b, dims=NN):
    return lax.dot_general(a, b, dims, preferred_element_type=F32)


def split3(x):
    hi = x.astype(BF16)
    rest = x - hi.astype(F32)
    mid = rest.astype(BF16)
    lo = (rest - mid.astype(F32)).astype(BF16)
    return jnp.concatenate([hi, mid, lo], axis=0)


def kernel(
    nf,
    nl,
    design,
    labels,
    ids,
    pri_col,
    pri_row,
    step_s,
    step_col,
    beta,
    pools,
    regions,
    beta_m,
    pool_m,
    region_m,
    beta_n,
    pools_n,
    regions_n,
    beta_mn,
    pool_mn,
    region_mn,
    mask,
    slope_t,
    slope,
    u2,
    dev,
    lik,
    term,
    part,
    rs_buf,
    resid,
    resid_f,
    xt_buf,
    reg_part,
    reg_buf,
    reg_own,
    reg_all,
    s_rs,
    r_rs,
    s_ag,
    r_ag,
    s_xt,
    r_xt,
    s_rr,
    r_rr,
    s_ra,
    r_ra,
):
    fi = lax.axis_index("feat")
    li = lax.axis_index("loan")
    chains = beta.shape[0]
    feats = design.shape[1]
    owned = pools.shape[1]
    g_own = pools.shape[2]
    n_reg = regions.shape[1]
    width = labels.shape[2]
    per = chains // nl
    stride = feats // g_own
    total_feats = float(feats * nf)

    def at(axis, n, i, k):
        return lax.rem(i + k, n)

    barrier = pltpu.get_barrier_semaphore()
    for k in range(1, nf):
        pl.semaphore_signal(
            barrier, inc=1, device_id={"feat": at("feat", nf, fi, k)}, device_id_type=MESH
        )
    for k in range(1, nl):
        pl.semaphore_signal(
            barrier, inc=1, device_id={"loan": at("loan", nl, li, k)}, device_id_type=MESH
        )

    def rows(j):
        return design[pl.ds(pl.multiple_of(j * width, width), width), :]

    def remote(src, dst, ss, rs, axis, peer):
        return pltpu.make_async_remote_copy(
            src_ref=src,
            dst_ref=dst,
            send_sem=ss,
            recv_sem=rs,
            device_id={axis: peer},
            device_id_type=MESH,
        )

    def rs_copy(t, k):
        peer = lax.rem(fi + k, nf)
        return remote(
            part.at[t, peer], rs_buf.at[t, k - 1], s_rs.at[t, k - 1], r_rs.at[t, k - 1], "feat", peer
        )

    def ag_copy(t, k, slot):
        peer = lax.rem(fi + k, nf)
        return remote(
            resid.at[t, slot], resid.at[t, slot], s_ag.at[t, k - 1], r_ag.at[t, k - 1], "feat", peer
        )

    def xt_copy(t, k):
        peer = lax.rem(li + k, nl)
        return remote(
            xt_buf.at[t, 0], xt_buf.at[t, k], s_xt.at[t, k - 1], r_xt.at[t, k - 1], "loan", peer
        )

    def rr_copy(t, k):
        peer = lax.rem(li + k, nl)
        return remote(
            reg_part.at[t, pl.ds(peer * per, per)],
            reg_buf.at[t, k - 1],
            s_rr.at[t, k - 1],
            r_rr.at[t, k - 1],
            "loan",
            peer,
        )

    def ra_copy(t, k, owner):
        peer = lax.rem(li + k, nl)
        return remote(
            reg_own.at[t],
            reg_all.at[t, owner],
            s_ra.at[t, k - 1],
            r_ra.at[t, k - 1],
            "loan",
            peer,
        )

    oh = (pri_col[...] == lax.broadcasted_iota(jnp.int32, (owned, n_reg), 1)).astype(F32)
    oh3 = jnp.concatenate([oh, oh, oh], axis=1).astype(BF16)
    oht = (pri_row[...] == lax.broadcasted_iota(jnp.int32, (n_reg, owned), 0)).astype(F32)
    oht3 = jnp.concatenate([oht, oht, oht], axis=1).astype(BF16)

    def region_dev(t, u_ref, v_ref):
        for c in range(chains):
            d = PREC * (u_ref[c] - dot(oh3, split3(v_ref[c])))
            dev[c] = d
            reg_part[t, c] = dot(oht3, split3(d))
        for k in range(1, nl):
            rr_copy(t, k).start()

    def region_reduce(t):
        for k in range(1, nl):
            rr_copy(t, k).wait_recv()
        total = reg_part[t, pl.ds(li * per, per)]
        for k in range(1, nl):
            total = total + reg_buf[t, k - 1]
        reg_own[t] = total
        for k in range(1, nl):
            ra_copy(t, k, li).start()
        reg_all[t, li] = total

    def region_gather(t):
        for k in range(1, nl):
            ra_copy(t, k, lax.rem(li + nl - k, nl)).wait_recv()

    def pool_terms(u_ref):
        for c in range(chains):
            u = u_ref[c]
            hi = u.astype(BF16).astype(F32)
            both = jnp.concatenate([hi, u - hi], axis=1)
            u2[pl.ds(c * owned, owned), :] = both.astype(BF16)

        def chunk(j, carry):
            z = dot(u2[...], slope_t[j])
            m = mask[j]
            for c in range(chains):
                term[j, pl.ds(c, 1), :] = jnp.sum(
                    z[c * owned : (c + 1) * owned] * m, axis=0, keepdims=True
                )
            return carry

        lax.fori_loop(0, nf, chunk, 0)

    def logits(t, b_ref):
        b16 = b_ref[...].astype(BF16)

        def chunk(j, carry):
            part[t, j] = term[j] + dot(b16, rows(j), NT)
            return carry

        lax.fori_loop(0, nf, chunk, 0)
        for k in range(1, nf):
            rs_copy(t, k).start()

    def residuals(t):
        for k in range(1, nf):
            rs_copy(t, k).wait_recv()
        logit = part[t, fi]
        for k in range(1, nf):
            logit = logit + rs_buf[t, k - 1]
        mine = (labels[fi].astype(F32) - jax.nn.sigmoid(logit)).astype(BF16)
        resid[t, fi] = mine
        for k in range(1, nf):
            ag_copy(t, k, fi).start()

    def population(t):
        total = dot(resid[t, fi], rows(fi))
        for k in range(1, nf):
            source = lax.rem(fi + nf - k, nf)
            ag_copy(t, k, source).wait_recv()
            total = total + dot(resid[t, source], rows(source))
        xt_buf[t, 0] = total
        for k in range(1, nl):
            xt_copy(t, k).start()

    def population_sum(t):
        for k in range(1, nl):
            xt_copy(t, k).wait_recv()
        total = xt_buf[t, li]
        for j in range(1, nl):
            total = total + xt_buf[t, lax.rem(li + nl - j, nl)]
        return total

    def likelihood(t):
        resid_f[...] = resid[t].astype(F32)
        lik[...] = jnp.zeros_like(lik)

        def chunk(j, carry):
            m = mask[j]
            a = jnp.concatenate(
                [(resid_f[j, pl.ds(c, 1), :] * m).astype(BF16) for c in range(chains)], axis=0
            )
            lik[...] += dot(a, slope[j])
            return carry

        lax.fori_loop(0, nf, chunk, 0)

    pick_t = (
        lax.broadcasted_iota(jnp.int32, (g_own, feats), 1)
        == stride * lax.broadcasted_iota(jnp.int32, (g_own, feats), 0)
    ).astype(F32).astype(BF16)
    first = li * owned

    def prepare(j, carry):
        x = rows(j)
        st = dot(pick_t, x, NT).astype(BF16)
        slope_t[j] = jnp.concatenate([st, st], axis=0)
        slope[j] = dot(x, pick_t, NT).astype(BF16)
        mask[j] = (
            ids[j] - first == lax.broadcasted_iota(jnp.int32, (owned, width), 0)
        ).astype(F32)
        return carry

    lax.fori_loop(0, nf, prepare, 0)
    half = 0.5 * step_col[...]

    pool_terms(pools)
    pl.semaphore_wait(barrier, nf + nl - 2)
    logits(0, beta)
    region_dev(0, pools, regions)
    residuals(0)
    region_reduce(0)
    population(0)
    likelihood(0)
    for c in range(chains):
        e = step_s[c]
        m = pool_m[c] + (0.5 * e) * (lik[pl.ds(c * owned, owned), :] - dev[c])
        pool_mn[c] = m
        pools_n[c] = pools[c] + e * m
    region_gather(0)
    for c in range(chains):
        e = step_s[c]
        g = reg_all[0, c // per, c % per] - PREC * regions[c]
        m = region_m[c] + (0.5 * e) * g
        region_mn[c] = m
        regions_n[c] = regions[c] + e * m
    region_dev(1, pools_n, regions_n)
    pool_terms(pools_n)
    mb = beta_m[...] + half * (population_sum(0) - total_feats * beta[...])
    beta_mn[...] = mb
    beta_n[...] = beta[...] + step_col[...] * mb
    logits(1, beta_n)
    region_reduce(1)
    residuals(1)
    population(1)
    likelihood(1)
    for c in range(chains):
        pool_mn[c] = pool_mn[c] + (0.5 * step_s[c]) * (lik[pl.ds(c * owned, owned), :] - dev[c])
    region_gather(1)
    for c in range(chains):
        g = reg_all[1, c // per, c % per] - PREC * regions_n[c]
        region_mn[c] = region_mn[c] + (0.5 * step_s[c]) * g
    beta_mn[...] = beta_mn[...] + half * (population_sum(1) - total_feats * beta_n[...])
    for t in range(2):
        for k in range(1, nf):
            rs_copy(t, k).wait_send()
            ag_copy(t, k, fi).wait_send()
        for k in range(1, nl):
            xt_copy(t, k).wait_send()
            rr_copy(t, k).wait_send()
            ra_copy(t, k, li).wait_send()


def body(
    nf,
    nl,
    design,
    labels,
    pool_ids,
    pool_region_index,
    step_size,
    beta,
    pools,
    regions,
    beta_momentum,
    pool_momentum,
    region_momentum,
):
    loans, feats = design.shape
    chains, owned, g_own = pools.shape
    n_reg = regions.shape[1]
    width = loans // nf
    per = chains // nl
    vmem = pl.BlockSpec(memory_space=pltpu.VMEM)
    smem = pl.BlockSpec(memory_space=pltpu.SMEM)
    dma = pltpu.SemaphoreType.DMA
    args = (
        design,
        labels.reshape(nf, 1, width),
        pool_ids.reshape(nf, 1, width),
        pool_region_index.reshape(owned, 1),
        pool_region_index.reshape(1, owned),
        step_size,
        step_size.reshape(chains, 1),
        beta,
        pools,
        regions,
        beta_momentum,
        pool_momentum,
        region_momentum,
    )
    outs = (beta, pools, regions, beta_momentum, pool_momentum, region_momentum)
    return pl.pallas_call(
        functools.partial(kernel, nf, nl),
        out_shape=tuple(jax.ShapeDtypeStruct(x.shape, x.dtype) for x in outs),
        in_specs=[smem if i == 5 else vmem for i in range(len(args))],
        out_specs=tuple(vmem for _ in outs),
        scratch_shapes=[
            pltpu.VMEM((nf, owned, width), F32),
            pltpu.VMEM((nf, 2 * g_own, width), BF16),
            pltpu.VMEM((nf, width, g_own), BF16),
            pltpu.VMEM((chains * owned, 2 * g_own), BF16),
            pltpu.VMEM((chains, owned, g_own), F32),
            pltpu.VMEM((chains * owned, g_own), F32),
            pltpu.VMEM((nf, chains, width), F32),
            pltpu.VMEM((2, nf, chains, width), F32),
            pltpu.VMEM((2, nf - 1, chains, width), F32),
            pltpu.VMEM((2, nf, chains, width), BF16),
            pltpu.VMEM((nf, chains, width), F32),
            pltpu.VMEM((2, nl, chains, feats), F32),
            pltpu.VMEM((2, chains, n_reg, g_own), F32),
            pltpu.VMEM((2, nl - 1, per, n_reg, g_own), F32),
            pltpu.VMEM((2, per, n_reg, g_own), F32),
            pltpu.VMEM((2, nl, per, n_reg, g_own), F32),
            dma((2, nf - 1)),
            dma((2, nf - 1)),
            dma((2, nf - 1)),
            dma((2, nf - 1)),
            dma((2, nl - 1)),
            dma((2, nl - 1)),
            dma((2, nl - 1)),
            dma((2, nl - 1)),
            dma((2, nl - 1)),
            dma((2, nl - 1)),
        ],
        compiler_params=pltpu.CompilerParams(
            collective_id=0, has_side_effects=True, vmem_limit_bytes=60 << 20
        ),
    )(*args)


def solution(mesh):
    in_specs = (
        P(("grp", "loan"), "feat"),
        P(("grp", "loan")),
        P(("grp", "loan")),
        P(("grp", "loan")),
        P("grp"),
        P("grp", "feat"),
        P("grp", "loan", "feat"),
        P("grp", None, "feat"),
        P("grp", "feat"),
        P("grp", "loan", "feat"),
        P("grp", None, "feat"),
    )
    out_specs = (
        P("grp", "feat"),
        P("grp", "loan", "feat"),
        P("grp", None, "feat"),
        P("grp", "feat"),
        P("grp", "loan", "feat"),
        P("grp", None, "feat"),
    )
    step = functools.partial(body, mesh.shape["feat"], mesh.shape["loan"])
    return jax.shard_map(step, mesh=mesh, in_specs=in_specs, out_specs=out_specs, check_vma=False)
```

time: 295 us -> 88.5 us (0.30)
  waiting for transfers between devices: 113 us -> 0 us
  Pallas kernels: 0 us -> 74.2 us
  local copies, waits for them, and re-layouts: 84.2 us -> 13.2 us
  other arithmetic: 49.3 us -> 0 us
  matrix products: 23.1 us -> 0 us
  between operations: 14 us -> 0.64 us
  blocking collectives: 10.5 us -> 0 us
    psum x2 -> x0, waiting for transfers between devices: 75.6 us -> none  [gradient(): xt_total, region_total = lax.psum((xt, region_part), 'loan')]
    pallas_call x0 -> x1, Pallas kernels: none -> 74.2 us  [body(): pl.pallas_call(functools.partial(kernel, nf, nl), out_shape=tuple((jax.Sh...]
    gather x2 -> x0, local copies, waits for them, and re-layouts: 71 us -> none  [gradient(): chosen = jnp.take(upper_operand, local_ids, axis=1)]
    reduce_scatter x2 -> x0, waiting for transfers between devices: 37.4 us -> none  [gradient(): lax.psum_scatter(partial_logit, 'feat', scatter_dimension=1, tiled=True)]
    unnamed x1 -> x0, other arithmetic: 32.8 us -> none
    dot_general x10 -> x0, matrix products: 23.1 us -> none  [the longest x2 6.95 us: gradient(): lax.dot_general(resid, design, (((1,), (0,)), ((), ())), preferred_elemen...]
    slice x1 -> x0, local copies, waits for them, and re-layouts: 11.7 us -> none  [gradient(): slope_bf = design[:, ::stride]]
    all_gather x2 -> x0, blocking collectives: 10.5 us -> none  [gradient(): resid = lax.all_gather(resid_share, 'feat', axis=1, tiled=True)]
  transfers between devices with their start and end apart: 4 -> 0, of which waited for: 4 -> 0; matrix products, arithmetic and copies ran while one was open for 3% -> 0% of each run, Pallas kernels for 0% -> 0%
where the time goes in v1:
time: 88.5 us; the launch traced here: 88.1 us
  Pallas kernels  74.2 us (84%)
  local copies, waits for them, and re-layouts  13.2 us (15%)
    pallas_call x1, Pallas kernels, body(): pl.pallas_call(functools.partial(kernel, nf, nl), out_shape=tuple((jax.Sh...  74.2 us
    unnamed x6, local copies, waits for them, and re-layouts  10.5 us

profile of v1, /device:TPU:0, one launch (start us, length us, event | category | flops | bytes accessed | tf_op | source)
XLA Modules:
  0.0 88.1 jit_solution(7828766543798924545)
XLA Ops:
  0.6 1.3 %copy.18.step_col = f32[16,1]{1,0:T(8,128)} copy(f32[16,1]{0,1:T(1,128)} %bitcast.9) | data formatting | bytes 128 | tf_op jit(solution)/shard_map/reshape | solution.py:353
  2.0 1.4 %copy.17.pri_col = s32[64,1]{1,0:T(8,128)} copy(s32[64,1]{0,1:T(1,128)} %bitcast.7) | data formatting | bytes 512 | tf_op jit(solution)/shard_map/reshape | solution.py:350
  3.3 74.2 %shard_map.154 = (f32[16,1024]{1,0:T(8,128)}, f32[16,64,64]{2,1,0:T(8,128)}, f32[16,64,64]{2,1,0:T(8,128)}, f32[16,1024]{1,0:T(8,128)}, f32[16,64,64]{2,1,0:T(8,128)}, /*index=5*/f32[16,64,64]{2,1,0:T(8,128)}) custom-call(bf16[2048,1024]{1,0:T(8,128)(2,1)} %design.1, s32[4,1,512]{2,1,0:T(1,128)} %bitcast.5, s32[4,1,512]{2,1,0:T(1,128)} %bitcast.6, ...), custom_call_target="tpu_custom_call" | custom-call | tf_op jit(solution)/shard_map/pallas_call | solution.py:362
  77.6 1.5 %copy.25 = f32[16,1024]{1,0:T(8,128)} copy(f32[16,1024]{1,0:T(8,128)} %get-tuple-element.12) | data formatting | bytes 131072
  79.1 1.9 %copy.26 = f32[16,64,64]{2,1,0:T(8,128)} copy(f32[16,64,64]{2,1,0:T(8,128)} %get-tuple-element.13) | data formatting | bytes 524288
  80.9 1.9 %copy.27 = f32[16,64,64]{2,1,0:T(8,128)} copy(f32[16,64,64]{2,1,0:T(8,128)} %get-tuple-element.14) | data formatting | bytes 524288
  82.8 1.5 %copy.28 = f32[16,1024]{1,0:T(8,128)} copy(f32[16,1024]{1,0:T(8,128)} %get-tuple-element.15) | data formatting | bytes 131072
  84.3 1.9 %copy.29 = f32[16,64,64]{2,1,0:T(8,128)} copy(f32[16,64,64]{2,1,0:T(8,128)} %get-tuple-element.16) | data formatting | bytes 524288
  86.2 1.9 %copy.30 = f32[16,64,64]{2,1,0:T(8,128)} copy(f32[16,64,64]{2,1,0:T(8,128)} %get-tuple-element.17) | data formatting | bytes 524288

commit v2 on v1

--- a/solution.py
+++ b/solution.py
@@ -30,13 +30,11 @@
 def kernel(
     nf,
     nl,
-    design,
+    design_hbm,
     labels,
     ids,
-    pri_col,
     pri_row,
     step_s,
-    step_col,
     beta,
     pools,
     regions,
@@ -49,6 +47,7 @@
     beta_mn,
     pool_mn,
     region_mn,
+    design,
     mask,
     slope_t,
     slope,
@@ -65,6 +64,7 @@
     reg_buf,
     reg_own,
     reg_all,
+    load,
     s_rs,
     r_rs,
     s_ag,
@@ -91,6 +91,17 @@
     def at(axis, n, i, k):
         return lax.rem(i + k, n)
 
+    fetch = pltpu.make_async_copy(design_hbm, design, load)
+    fetch.start()
+    fold = folds(n_reg, g_own)
+    lines = n_reg // fold
+
+    def pack(x):
+        return jnp.concatenate([x[i * lines : (i + 1) * lines] for i in range(fold)], axis=1)
+
+    def unpack(x):
+        return jnp.concatenate([x[:, i * g_own : (i + 1) * g_own] for i in range(fold)], axis=0)
+
     barrier = pltpu.get_barrier_semaphore()
     for k in range(1, nf):
         pl.semaphore_signal(
@@ -154,16 +165,20 @@
             peer,
         )
 
-    oh = (pri_col[...] == lax.broadcasted_iota(jnp.int32, (owned, n_reg), 1)).astype(F32)
+    oht = (pri_row[...] == lax.broadcasted_iota(jnp.int32, (n_reg, owned), 0)).astype(F32)
+    eye = (
+        lax.broadcasted_iota(jnp.int32, (owned, owned), 0)
+        == lax.broadcasted_iota(jnp.int32, (owned, owned), 1)
+    ).astype(F32)
+    oh = dot(eye.astype(BF16), oht.astype(BF16), NT)
     oh3 = jnp.concatenate([oh, oh, oh], axis=1).astype(BF16)
-    oht = (pri_row[...] == lax.broadcasted_iota(jnp.int32, (n_reg, owned), 0)).astype(F32)
     oht3 = jnp.concatenate([oht, oht, oht], axis=1).astype(BF16)
 
     def region_dev(t, u_ref, v_ref):
         for c in range(chains):
             d = PREC * (u_ref[c] - dot(oh3, split3(v_ref[c])))
             dev[c] = d
-            reg_part[t, c] = dot(oht3, split3(d))
+            reg_part[t, c] = pack(dot(oht3, split3(d)))
         for k in range(1, nl):
             rr_copy(t, k).start()
 
@@ -270,15 +285,20 @@
         ).astype(F32)
         return carry
 
+    chain = lax.broadcasted_iota(jnp.int32, (chains, 1), 0)
+    step_col = jnp.zeros((chains, 1), F32)
+    for c in range(chains):
+        step_col = jnp.where(chain == c, step_s[c], step_col)
+    half = 0.5 * step_col
+
+    pl.semaphore_wait(barrier, nf + nl - 2)
+    region_dev(0, pools, regions)
+    fetch.wait()
     lax.fori_loop(0, nf, prepare, 0)
-    half = 0.5 * step_col[...]
-
     pool_terms(pools)
-    pl.semaphore_wait(barrier, nf + nl - 2)
     logits(0, beta)
-    region_dev(0, pools, regions)
+    region_reduce(0)
     residuals(0)
-    region_reduce(0)
     population(0)
     likelihood(0)
     for c in range(chains):
@@ -289,7 +309,7 @@
     region_gather(0)
     for c in range(chains):
         e = step_s[c]
-        g = reg_all[0, c // per, c % per] - PREC * regions[c]
+        g = unpack(reg_all[0, c // per, c % per]) - PREC * regions[c]
         m = region_m[c] + (0.5 * e) * g
         region_mn[c] = m
         regions_n[c] = regions[c] + e * m
@@ -297,7 +317,7 @@
     pool_terms(pools_n)
     mb = beta_m[...] + half * (population_sum(0) - total_feats * beta[...])
     beta_mn[...] = mb
-    beta_n[...] = beta[...] + step_col[...] * mb
+    beta_n[...] = beta[...] + step_col * mb
     logits(1, beta_n)
     region_reduce(1)
     residuals(1)
@@ -307,7 +327,7 @@
         pool_mn[c] = pool_mn[c] + (0.5 * step_s[c]) * (lik[pl.ds(c * owned, owned), :] - dev[c])
     region_gather(1)
     for c in range(chains):
-        g = reg_all[1, c // per, c % per] - PREC * regions_n[c]
+        g = unpack(reg_all[1, c // per, c % per]) - PREC * regions_n[c]
         region_mn[c] = region_mn[c] + (0.5 * step_s[c]) * g
     beta_mn[...] = beta_mn[...] + half * (population_sum(1) - total_feats * beta_n[...])
     for t in range(2):
@@ -318,6 +338,16 @@
             xt_copy(t, k).wait_send()
             rr_copy(t, k).wait_send()
             ra_copy(t, k, li).wait_send()
+
+
+def folds(n_reg, g_own):
+    return max(1, min(128 // g_own, n_reg // 8))
+
+
+def emit(*refs):
+    n = len(refs) // 2
+    for i in range(n):
+        refs[n + i][...] = refs[i][...]
 
 
 def body(
@@ -339,18 +369,19 @@
     chains, owned, g_own = pools.shape
     n_reg = regions.shape[1]
     width = loans // nf
+    fold = folds(n_reg, g_own)
+    packed = (n_reg // fold, fold * g_own)
     per = chains // nl
     vmem = pl.BlockSpec(memory_space=pltpu.VMEM)
     smem = pl.BlockSpec(memory_space=pltpu.SMEM)
+    hbm = pl.BlockSpec(memory_space=pl.ANY)
     dma = pltpu.SemaphoreType.DMA
     args = (
         design,
         labels.reshape(nf, 1, width),
         pool_ids.reshape(nf, 1, width),
-        pool_region_index.reshape(owned, 1),
         pool_region_index.reshape(1, owned),
         step_size,
-        step_size.reshape(chains, 1),
         beta,
         pools,
         regions,
@@ -359,12 +390,14 @@
         region_momentum,
     )
     outs = (beta, pools, regions, beta_momentum, pool_momentum, region_momentum)
-    return pl.pallas_call(
+    shapes = tuple(jax.ShapeDtypeStruct(x.shape, x.dtype) for x in outs)
+    results = pl.pallas_call(
         functools.partial(kernel, nf, nl),
-        out_shape=tuple(jax.ShapeDtypeStruct(x.shape, x.dtype) for x in outs),
-        in_specs=[smem if i == 5 else vmem for i in range(len(args))],
+        out_shape=shapes,
+        in_specs=[{0: hbm, 4: smem}.get(i, vmem) for i in range(len(args))],
         out_specs=tuple(vmem for _ in outs),
         scratch_shapes=[
+            pltpu.VMEM((loans, feats), BF16),
             pltpu.VMEM((nf, owned, width), F32),
             pltpu.VMEM((nf, 2 * g_own, width), BF16),
             pltpu.VMEM((nf, width, g_own), BF16),
@@ -377,10 +410,11 @@
             pltpu.VMEM((2, nf, chains, width), BF16),
             pltpu.VMEM((nf, chains, width), F32),
             pltpu.VMEM((2, nl, chains, feats), F32),
-            pltpu.VMEM((2, chains, n_reg, g_own), F32),
-            pltpu.VMEM((2, nl - 1, per, n_reg, g_own), F32),
-            pltpu.VMEM((2, per, n_reg, g_own), F32),
-            pltpu.VMEM((2, nl, per, n_reg, g_own), F32),
+            pltpu.VMEM((2, chains) + packed, F32),
+            pltpu.VMEM((2, nl - 1, per) + packed, F32),
+            pltpu.VMEM((2, per) + packed, F32),
+            pltpu.VMEM((2, nl, per) + packed, F32),
+            dma,
             dma((2, nf - 1)),
             dma((2, nf - 1)),
             dma((2, nf - 1)),
@@ -396,6 +430,12 @@
             collective_id=0, has_side_effects=True, vmem_limit_bytes=60 << 20
         ),
     )(*args)
+    return pl.pallas_call(
+        emit,
+        out_shape=shapes,
+        in_specs=[vmem] * len(shapes),
+        out_specs=tuple(vmem for _ in shapes),
+    )(*results)
 
 
 def solution(mesh):

time: 88.5 us -> 49.4 us (0.56)
  Pallas kernels: 74.2 us -> 48.6 us
  local copies, waits for them, and re-layouts: 13.2 us -> 0 us
    pallas_call x1 -> x2, Pallas kernels: 74.2 us -> 48.6 us  [the longest x1 45.7 us: body(): pl.pallas_call(functools.partial(kernel, nf, nl), out_shape=shapes, in_sp...]
    unnamed x6 -> x0, local copies, waits for them, and re-layouts: 10.5 us -> none
    reshape x2 -> x0, local copies, waits for them, and re-layouts: 2.69 us -> none  [the longest x1 1.36 us: body(): pool_region_index.reshape(owned, 1)]
where the time goes in v2:
time: 49.4 us; the launch traced here: 49.3 us
  Pallas kernels  48.6 us (98%)
  between operations  0.64 us (1%)
    pallas_call x1, Pallas kernels, body(): pl.pallas_call(functools.partial(kernel, nf, nl), out_shape=shapes, in_sp...  45.7 us
    pallas_call x1, Pallas kernels, body(): pl.pallas_call(emit, out_shape=shapes, in_specs=[vmem] * len(shapes), out...  2.95 us

profile of v2, /device:TPU:0, one launch (start us, length us, event | category | flops | bytes accessed | tf_op | source)
XLA Modules:
  0.0 49.3 jit_solution(15984551990605748)
XLA Ops:
  0.6 45.7 %shard_map.154 = (f32[16,1024]{1,0:T(8,128)}, f32[16,64,64]{2,1,0:T(8,128)}, f32[16,64,64]{2,1,0:T(8,128)}, f32[16,1024]{1,0:T(8,128)}, f32[16,64,64]{2,1,0:T(8,128)}, /*index=5*/f32[16,64,64]{2,1,0:T(8,128)}) custom-call(bf16[2048,1024]{1,0:T(8,128)(2,1)} %design_hbm.1, s32[4,1,512]{2,1,0:T(1,128)} %bitcast.3, s32[4,1,512]{2,1,0:T(1,128)} %bitcast.4, ...), custom_call_target="tpu_custom_call" | custom-call | tf_op jit(solution)/shard_map/pallas_call | solution.py:394
  46.3 2.9 %shard_map.155 = (f32[16,1024]{1,0:T(8,128)}, f32[16,64,64]{2,1,0:T(8,128)}, f32[16,64,64]{2,1,0:T(8,128)}, f32[16,1024]{1,0:T(8,128)}, f32[16,64,64]{2,1,0:T(8,128)}, /*index=5*/f32[16,64,64]{2,1,0:T(8,128)}) custom-call(f32[16,1024]{1,0:T(8,128)} %get-tuple-element.12.refs_0_, f32[16,64,64]{2,1,0:T(8,128)} %get-tuple-element.13.refs_1_, ...), custom_call_target="tpu_custom_call" | custom-call | tf_op jit(solution)/shard_map/pallas_call | solution.py:433
